TPU v7x, 256 devices: a whole 4x4x8 slice. The times are simulated.
256 devices in a mesh: silo: 32 (over z, y_lo, core), shard: 8 (over x, y_hi).
Axes of the slice: x: 4, y: 4 (y_hi: 2, y_lo: 2; y = y_hi * 2 + y_lo), z: 8, core: 2. Of those that a mesh axis runs over, the one named last changes fastest.
Arguments:
- activ: bfloat16 [262144, 1280], P(('silo', 'shard')), may hold values from -6 to 6
- cotangent: bfloat16 [262144, 640], P(('silo', 'shard')), may hold values from -6 to 6
- error_memory: float32 [32, 8, 3200, 256], P('silo', 'shard'), may hold values from -5 to 5
- params: float32 [32, 640, 1280], P('silo', 'shard'), may hold values from -6 to 6
- estimate: float32 [32, 640, 1280], P('silo', 'shard'), may hold values from -6 to 6
- mixed: float32 [32, 640, 1280], P('silo', 'shard'), may hold values from -6 to 6
- kept_blocks: int32 [32, 8, 8, 64], P('silo'), may hold values from 0 to 399, as said below
- kept_counts: int32 [32, 8, 8], P('silo'), may hold values from 1 to 64, as said below
- gossip_blocks: int32 [32, 8, 128], P(None, 'shard'), may hold values from 0 to 399, as said below
- gossip_counts: int32 [32, 8], P(None, 'shard'), may hold values from 1 to 128, as said below
Outputs:
- params_out: float32 [32, 640, 1280], P('silo', 'shard')
- estimate_out: float32 [32, 640, 1280], P('silo', 'shard')
- mixed_out: float32 [32, 640, 1280], P('silo', 'shard')
- error_out: float32 [32, 8, 3200, 256], P('silo', 'shard')
Inputs may be any that keep to these rules, and one draw needn't show every extreme that they name: `kept_blocks`: for each silo, sender and owner the 64 entries are distinct. In every silo some owner has kept_counts equal to 64 from every sender. `kept_counts`: in every silo one owner receives 64 from every device of the silo. `gossip_blocks`: for each silo and owner the 128 entries are distinct. `gossip_counts`: for every owner some silo gossips 128 blocks.
All inputs are finite; a program needn't handle non-finite values.
Results may differ from a plain program's by a relative error of at most 0.0003.
Values sent between devices are 32-bit elements; how exact they have to be, the bound alone decides.
A program may use at most 64 MiB of HBM per device.

v0:
```python
import jax
import jax.numpy as jnp
from jax import lax
from jax.sharding import PartitionSpec as P

LEARN_RATE = 0.25
CONSENSUS = 0.5
MIX_WEIGHT = 1.0 / 3.0


def shifted(value, axis, steps):
    count = lax.axis_size(axis)
    pairs = [(source, (source + steps) % count) for source in range(count)]
    return lax.ppermute(value, axis, pairs)


def body(
    activ,
    cotangent,
    error_memory,
    params,
    estimate,
    mixed,
    kept_blocks,
    kept_counts,
    gossip_blocks,
    gossip_counts,
):
    shards = lax.axis_size("shard")
    my_shard = lax.axis_index("shard")
    my_silo = lax.axis_index("silo")
    width_in = activ.shape[1]
    block_len = error_memory.shape[3]
    nblocks = error_memory.shape[2]
    own_blocks = nblocks // shards
    slot_count = kept_blocks.shape[3]
    gossip_slots = gossip_blocks.shape[2]
    scale_in = width_in ** (-0.5)
    grad_local = (
        lax.dot_general(
            cotangent, activ, (((0,), (0,)), ((), ())), preferred_element_type=jnp.float32
        )
        * scale_in
    )
    pending = error_memory[0, 0] + grad_local.reshape(nblocks, block_len)
    my_lists = kept_blocks[0][my_shard]
    my_counts = kept_counts[0][my_shard]
    offsets = (jnp.arange(shards, dtype=jnp.int32) * own_blocks)[:, None]
    global_ids = my_lists + offsets
    filled = jnp.arange(slot_count, dtype=jnp.int32)[None, :] < my_counts[:, None]
    chosen = (
        jnp.zeros((nblocks,), jnp.int32)
        .at[global_ids.reshape(-1)]
        .max(filled.astype(jnp.int32).reshape(-1))
    )
    keep_mask = chosen[:, None] > 0
    error_new = jnp.where(keep_mask, jnp.float32(0.0), pending)
    slot_rows = jnp.where(filled[:, :, None], pending[global_ids], jnp.float32(0.0))
    arrived = lax.all_to_all(slot_rows, "shard", split_axis=0, concat_axis=0, tiled=True)
    source_lists = kept_blocks[0][:, my_shard]
    own_grad = (
        jnp.zeros((own_blocks, block_len), jnp.float32)
        .at[source_lists.reshape(-1)]
        .add(arrived.reshape(-1, block_len))
    )
    weights = params[0].reshape(own_blocks, block_len)
    half_step = weights - LEARN_RATE * own_grad
    old_estimate = estimate[0].reshape(own_blocks, block_len)
    drift = half_step - old_estimate
    silo_lists = gossip_blocks[:, 0]
    silo_counts = gossip_counts[:, 0]
    my_blocks = silo_lists[my_silo]
    gossip_filled = jnp.arange(gossip_slots, dtype=jnp.int32) < silo_counts[my_silo]
    delta_rows = jnp.where(gossip_filled[:, None], drift[my_blocks], jnp.float32(0.0))
    delta_dense = jnp.zeros_like(drift).at[my_blocks].set(delta_rows)
    estimate_new = old_estimate + delta_dense
    dense_lower = shifted(delta_dense, "silo", 1)
    dense_upper = shifted(delta_dense, "silo", -1)
    spread = delta_dense + dense_lower + dense_upper
    mixed_new = mixed[0].reshape(own_blocks, block_len) + MIX_WEIGHT * spread
    params_new = half_step + CONSENSUS * (mixed_new - estimate_new)
    return (
        params_new.reshape(params.shape),
        estimate_new.reshape(estimate.shape),
        mixed_new.reshape(mixed.shape),
        error_new.reshape(error_memory.shape),
    )


def solution(mesh):
    in_specs = (
        P(("silo", "shard"), None),
        P(("silo", "shard"), None),
        P("silo", "shard", None, None),
        P("silo", "shard", None),
        P("silo", "shard", None),
        P("silo", "shard", None),
        P("silo", None, None, None),
        P("silo", None, None),
        P(None, "shard", None),
        P(None, "shard"),
    )
    out_specs = (
        P("silo", "shard", None),
        P("silo", "shard", None),
        P("silo", "shard", None),
        P("silo", "shard", None, None),
    )
    return jax.shard_map(body, mesh=mesh, in_specs=in_specs, out_specs=out_specs, check_vma=False)
```

profile of v0, /device:TPU:17, one launch (start us, length us, event | category | flops | bytes accessed | tf_op | source)
XLA Modules:
  0.0 74.2 jit_solution(17001546863899442940)
XLA Ops:
  0.6 0.0 copy-start
  0.7 0.9 %compare_select_fusion.2 = (s32[8,64,1]{1,0,2:T(8,128)S(1)}, s32[1,1,8,64]{3,2,1,0:T(8,128)S(1)}) fusion(s32[8]{0:T(128)S(1)} %iota_multiply_fusion, s32[1,8,8,64]{3,2,1,0:T(8,128)} %param.16, s32[]{:T(128)S(6)} %select_n.63), kind=kLoop, calls=%fused_computation.22 | loop fusion | flops 2048 | bytes 6180 | tf_op jit(solution)/shard_map/select_n | solution.py:58
  1.6 0.1 reshape.216
  1.7 0.7 copy-done
  2.4 4.9 %convolution_multiply_fusion = f32[640,1280]{1,0:T(8,128)} fusion(bf16[1024,640]{1,0:T(8,128)(2,1)} %param.11, bf16[1024,1280]{1,0:T(8,128)(2,1)S(1)} %copy-done), kind=kOutput, calls=%fused_computation.5 | convolution fusion | flops 1678540800 | bytes 7208960 | tf_op jit(solution)/shard_map/dot_general | solution.py:40
  7.3 4.9 %reshape.207 = f32[3200,256]{1,0:T(8,128)} reshape(f32[640,1280]{1,0:T(8,128)} %convolution_multiply_fusion) | data formatting | bytes 6553600 | tf_op jit(solution)/shard_map/reshape | solution.py:45
  12.2 0.7 fusion.10
  12.9 0.1 fusion.14
  12.9 5.0 %bitcast_add_fusion = f32[3200,256]{1,0:T(8,128)} fusion(f32[3200,256]{1,0:T(8,128)} %reshape.207, f32[1,1,3200,256]{3,2,1,0:T(8,128)} %param.12), kind=kLoop, calls=%fused_computation.6 | loop fusion | flops 819200 | bytes 9830400 | tf_op jit(solution)/shard_map/add | solution.py:45
  18.0 0.0 copy-start.2
  18.0 3.5 %gather_fusion = f32[512,256]{1,0:T(8,128)S(1)} fusion(f32[3200,256]{1,0:T(8,128)} %bitcast_add_fusion, s32[1024]{0:T(1024)S(1)} %pad_clamp_fusion.1), kind=kCustom, calls=%fused_computation | custom fusion | bytes 1050624 | tf_op jit(solution)/shard_map/gather | solution.py:58
  21.5 0.9 %broadcast_select_fusion = f32[8,64,256]{2,1,0:T(8,128)} fusion(f32[8,64,256]{2,1,0:T(8,128)S(1)} %bitcast.27, pred[8,64]{1,0:T(8,128)(4,1)S(1)} %get-tuple-element.10), kind=kLoop, calls=%fused_computation.11 | loop fusion | flops 131072 | bytes 1049088 | tf_op jit(solution)/shard_map/jit(_where)/select_n | solution.py:58
  22.4 6.7 %all-to-all-start = ((f32[8,64,256]{2,1,0:T(8,128)}), f32[8,64,256]{2,1,0:T(8,128)}, u32[]{:S(2)}, u32[]{:S(2)}) async-start(f32[8,64,256]{2,1,0:T(8,128)} %broadcast_select_fusion), calls=%async_computation | async-start | bytes 1048576 | tf_op jit(solution)/shard_map/all_to_all | solution.py:59
  29.1 0.7 fusion.12
  29.8 0.0 copy-done.2
  29.8 0.6 constant_dynamic-slice_fusion
  30.4 0.1 squeeze.23
  30.4 0.1 add.126
  30.5 0.1 add.127
  30.6 0.6 iota_compare_fusion.1
  31.3 0.0 copy-start.1
  31.3 4.9 %reshape.212 = f32[1,1,3200,256]{3,2,1,0:T(8,128)} reshape(f32[640,1280]{1,0:T(8,128)} %convolution_multiply_fusion) | data formatting | bytes 6553600 | tf_op jit(solution)/shard_map/reshape | solution.py:45
  36.2 0.8 %dynamic-slice_reduce_fusion = s32[8,64]{1,0:T(8,128)S(1)} fusion(s32[1,8,8,64]{3,2,1,0:T(8,128)} %param.16, s32[]{:T(128)S(6)} %select_n.63), kind=kLoop, calls=%fused_computation.30 | loop fusion | bytes 4100 | tf_op jit(solution)/shard_map/dynamic_slice | solution.py:60
  37.0 0.1 reshape_squeeze.13
  37.0 0.0 copy-done.1
  37.1 0.1 reshape_squeeze.12
  37.2 1.1 %reshape_squeeze.15 = f32[400,256]{1,0:T(8,128)S(1)} reshape(f32[1,80,1280]{2,1,0:T(8,128)} %param.14) | data formatting | bytes 819200 | tf_op jit(solution)/shard_map/reshape;squeeze | solution.py:68
  38.3 0.1 reshape.250
  38.4 3.8 %scatter_custom_fusion.2 = s32[3200]{0:T(1024)S(1)} fusion(s32[512]{0:T(512)S(1)} %bitcast.28, s32[512]{0:T(512)S(1)} %reshape.250, s32[]{:T(128)} %constant.14.clone.1), kind=kCustom, calls=%fused_computation.24 | custom fusion | flops 512 | bytes 12804 | tf_op jit(solution)/shard_map/scatter-max | solution.py:54
  42.2 0.0 all-to-all-done
  42.2 4.5 %scatter_custom_fusion = f32[400,256]{1,0:T(8,128)} fusion(s32[512]{0:T(512)S(1)} %bitcast.29, f32[512,256]{1,0:T(8,128)} %bitcast.5, f32[]{:T(128)} %constant.13.clone.1), kind=kCustom, calls=%fused_computation.14 | custom fusion | flops 131072 | bytes 410112 | tf_op jit(solution)/shard_map/scatter-add | solution.py:64
  46.8 1.8 %fusion.4 = f32[400,256]{1,0:T(8,128)} fusion(f32[400,256]{1,0:T(8,128)S(1)} %reshape_squeeze.15, f32[400,256]{1,0:T(8,128)S(1)} %reshape_squeeze.12, f32[400,256]{1,0:T(8,128)} %scatter_custom_fusion), kind=kLoop, calls=%fused_computation.16 | loop fusion | flops 307200 | bytes 1638400 | tf_op jit(solution)/shard_map/sub | solution.py:69
  48.6 3.2 %scatter_custom_fusion.1 = f32[400,256]{1,0:T(8,128)} fusion(s32[128]{0:T(128)S(1)} %fusion.12, f32[]{:T(128)} %constant.13.clone.1, pred[128]{0:T(512)(128)(4,1)S(1)} %iota_compare_fusion.1, f32[400,256]{1,0:T(8,128)} %fusion.4, s32[1024]{0:T(1024)S(1)} %pad_clamp_fusion), kind=kCustom, calls=%fused_computation.12 | custom fusion | flops 32768 | bytes 824832 | tf_op jit(solution)/shard_map/scatter | solution.py:75
  51.8 2.2 %collective-permute-start = (f32[400,256]{1,0:T(8,128)}, f32[400,256]{1,0:T(8,128)}, u32[]{:S(2)}, u32[]{:S(2)}) collective-permute-start(f32[400,256]{1,0:T(8,128)} %scatter_custom_fusion.1), channel_id=1, source_target_pairs={{0,8},{8,16},{16,24},{24,32},{32,40},{40,48},{48,56},{56,64},{64,7... | collective-permute-start | bytes 1228808 | tf_op jit(solution)/shard_map/ppermute | solution.py:14
  53.9 0.0 collective-permute-start.1
  53.9 4.9 %add_select_fusion = f32[1,1,3200,256]{3,2,1,0:T(8,128)} fusion(f32[1,1,3200,256]{3,2,1,0:T(8,128)} %param.12, f32[1,1,3200,256]{3,2,1,0:T(8,128)} %reshape.212, pred[3200]{0:T(1024)(128)(4,1)S(1)} %broadcast_compare_fusion), kind=kLoop, calls=%fused_computation.7 | loop fusion | flops 1638400 | bytes 9833600 | tf_op jit(solution)/shard_map/jit(_where)/select_n | solution.py:57
  58.8 1.9 %reshape_squeeze.14 = f32[400,256]{1,0:T(8,128)} reshape(f32[1,80,1280]{2,1,0:T(8,128)} %param.15) | data formatting | bytes 819200 | tf_op jit(solution)/shard_map/reshape;squeeze | solution.py:80
  60.7 2.9 %collective-permute-done = f32[400,256]{1,0:T(8,128)} collective-permute-done((f32[400,256]{1,0:T(8,128)}, f32[400,256]{1,0:T(8,128)}, u32[]{:S(2)}, u32[]{:S(2)}) %collective-permute-start) | collective-permute-done | bytes 409632 | tf_op jit(solution)/shard_map/ppermute | solution.py:14
  63.5 2.5 %collective-permute-done.1 = f32[400,256]{1,0:T(8,128)} collective-permute-done((f32[400,256]{1,0:T(8,128)}, f32[400,256]{1,0:T(8,128)}, u32[]{:S(2)}, u32[]{:S(2)}) %collective-permute-start.1) | collective-permute-done | bytes 409632 | tf_op jit(solution)/shard_map/ppermute | solution.py:14
  66.0 2.6 %multiply_add_fusion = (f32[400,256]{1,0:T(8,128)}, f32[400,256]{1,0:T(8,128)}, f32[400,256]{1,0:T(8,128)}) fusion(f32[400,256]{1,0:T(8,128)S(1)} %reshape_squeeze.12, f32[400,256]{1,0:T(8,128)} %scatter_custom_fusion, f32[400,256]{1,0:T(8,128)S(1)} %reshape_squeeze.15, f32[400,256]{1,0:T(8,128)} %scatter_custom_fusion.1, f32[400,256]{1,0:T(8,128)} %reshape_squeeze.14, ...), kind=kLoop, calls=%fused_computation.8 | loop fusion | flops 1024000 | bytes 4096000 | tf_op jit(solution)/shard_map/add | solution.py:81
  68.6 1.9 %reshape.209 = f32[1,80,1280]{2,1,0:T(8,128)} reshape(f32[400,256]{1,0:T(8,128)} %get-tuple-element.4) | data formatting | bytes 819200 | tf_op jit(solution)/shard_map/reshape | solution.py:83
  70.5 1.9 %reshape.210 = f32[1,80,1280]{2,1,0:T(8,128)} reshape(f32[400,256]{1,0:T(8,128)} %get-tuple-element.5) | data formatting | bytes 819200 | tf_op jit(solution)/shard_map/reshape | solution.py:84
  72.4 1.9 %reshape.211 = f32[1,80,1280]{2,1,0:T(8,128)} reshape(f32[400,256]{1,0:T(8,128)} %get-tuple-element.6) | data formatting | bytes 819200 | tf_op jit(solution)/shard_map/reshape | solution.py:85
  (6 shorter events, 0.0 us)
Async XLA Ops:
  0.6 1.8 %copy-start = (bf16[1024,1280]{1,0:T(8,128)(2,1)S(1)}, bf16[1024,1280]{1,0:T(8,128)(2,1)}, u32[]{:S(2)}) copy-start(bf16[1024,1280]{1,0:T(8,128)(2,1)} %param.10) | copy-start | bytes 7864324
  18.0 11.8 %copy-start.2 = (s32[32,1]{0,1:T(1,128)S(1)}, s32[32,1]{0,1:T(1,128)}, u32[]{:S(2)}) copy-start(s32[32,1]{0,1:T(1,128)} %param.19) | copy-start | bytes 388
  22.4 19.8 %all-to-all-start = ((f32[8,64,256]{2,1,0:T(8,128)}), f32[8,64,256]{2,1,0:T(8,128)}, u32[]{:S(2)}, u32[]{:S(2)}) async-start(f32[8,64,256]{2,1,0:T(8,128)} %broadcast_select_fusion), calls=%async_computation | async-start | bytes 1048576 | tf_op jit(solution)/shard_map/all_to_all | solution.py:59
  31.3 5.8 %copy-start.1 = (f32[1,80,1280]{2,1,0:T(8,128)S(1)}, f32[1,80,1280]{2,1,0:T(8,128)}, u32[]{:S(2)}) copy-start(f32[1,80,1280]{2,1,0:T(8,128)} %param.13) | copy-start | bytes 1228804
  51.8 11.8 %collective-permute-start = (f32[400,256]{1,0:T(8,128)}, f32[400,256]{1,0:T(8,128)}, u32[]{:S(2)}, u32[]{:S(2)}) collective-permute-start(f32[400,256]{1,0:T(8,128)} %scatter_custom_fusion.1), channel_id=1, source_target_pairs={{0,8},{8,16},{16,24},{24,32},{32,40},{40,48},{48,56},{56,64},{64,7... | collective-permute-start | bytes 1228808 | tf_op jit(solution)/shard_map/ppermute | solution.py:14
  53.9 12.1 %collective-permute-start.1 = (f32[400,256]{1,0:T(8,128)}, f32[400,256]{1,0:T(8,128)}, u32[]{:S(2)}, u32[]{:S(2)}) collective-permute-start(f32[400,256]{1,0:T(8,128)} %scatter_custom_fusion.1), channel_id=1, source_target_pairs={{0,248},{8,0},{16,8},{24,16},{32,24},{40,32},{48,40},{56,48},{64,5... | collective-permute-start | bytes 1228808 | tf_op jit(solution)/shard_map/ppermute | solution.py:14
where the time goes:
time: 75.1 us; the launch traced here: 74.2 us
  other arithmetic  29.1 us (39%)
  local copies, waits for them, and re-layouts  25.2 us (34%)
  starting transfers between devices  8.86 us (12%)
  waiting for transfers between devices  5.34 us (7%)
  matrix products  4.92 us (7%)
    reshape x2, local copies, waits for them, and re-layouts, body(): pending = error_memory[0, 0] + grad_local.reshape(nblocks, block_len)  9.78 us
    all_to_all x1, starting transfers between devices, body(): lax.all_to_all(slot_rows, 'shard', split_axis=0, concat_axis=0, tiled=True)  6.7 us
    ppermute x2, waiting for transfers between devices, shifted(): return lax.ppermute(value, axis, pairs)  5.34 us
    add x1, other arithmetic, body(): pending = error_memory[0, 0] + grad_local.reshape(nblocks, block_len)  5.03 us
    dot_general x1, matrix products, body(): lax.dot_general(cotangent, activ, (((0,), (0,)), ((), ())), preferred_ele...  4.92 us
    select_n x1, other arithmetic, body(): error_new = jnp.where(keep_mask, jnp.float32(0.0), pending)  4.88 us
    scatter-add x1, other arithmetic, body(): own_grad = jnp.zeros((own_blocks, block_len), jnp.float32).at[source_list...  4.52 us
    another operation x1, other arithmetic, body(): chosen = jnp.zeros((nblocks,), jnp.int32).at[global_ids.reshape(-1)].max(...  3.83 us
  transfers between devices with their start and end apart: 3, of which 2 were waited for; matrix products, arithmetic and copies ran while one was open for 27% of the time, Pallas kernels for 0%

commit v1 on v0

v1 whole, which is shorter than its diff:
```python
import functools

import jax
import jax.numpy as jnp
from jax import lax
from jax.experimental import pallas as pl
from jax.experimental.pallas import tpu as pltpu
from jax.sharding import PartitionSpec as P

LEARN_RATE = 0.25
CONSENSUS = 0.5
MIX_WEIGHT = 1.0 / 3.0
MESH = pl.DeviceIdType.MESH
LANES = 128


def split_pair(value):
    high = value.astype(jnp.bfloat16)
    low = (value - high.astype(jnp.float32)).astype(jnp.bfloat16)
    return high, low


def remote(src, dst, send, recv, target):
    return pltpu.make_async_remote_copy(
        src_ref=src, dst_ref=dst, send_sem=send, recv_sem=recv,
        device_id=target, device_id_type=MESH,
    )


def kernel(
    dims,
    activ_h, cot_h, mem_h, params_h, est_h, mixed_h, kept_h, kcnt_h, gos_h, gcnt_h,
    params_o, est_o, mixed_o, error_o,
    act_v, cot_v, cot_t, pend, slots, arrived, pieces, onehot, mask_own, gos_take, gos_put,
    drift_p, gos_send, gos_recv, gos_p, par_v, est_v, mix_v, kept_v, gos_v,
    kept_s, kcnt_s, gcnt_s,
    load_sem, send_sem, recv_sem, gsend_sem, grecv_sem,
):
    silos, shards, own, cap, gk, tiles, block = dims
    rows = own // tiles
    halves = block // LANES
    total_rows = rows * shards
    silo = lax.axis_index("silo")
    shard = lax.axis_index("shard")
    upper = lax.rem(silo + 1, silos)
    lower = lax.rem(silo + silos - 1, silos)
    scale = float(act_v.shape[1]) ** -0.5

    loads = []

    def load(src, dst):
        copy = pltpu.make_async_copy(src, dst, load_sem.at[len(loads)])
        copy.start()
        loads.append(copy)
        return copy

    load_cot = load(cot_h, cot_v)
    load_act = [
        load(activ_h.at[:, pl.ds(c * block, block)], act_v.at[:, pl.ds(c * block, block)])
        for c in range(tiles)
    ]
    load_mem = [load(mem_h.at[:, pl.ds(h * LANES, LANES)], pend.at[h]) for h in range(halves)]
    load_kept_s = load(kept_h.at[shard], kept_s)
    load_rest = [
        load(kept_h, kept_v),
        load(kcnt_h, kcnt_s),
        load(gos_h, gos_v),
        load(gcnt_h, gcnt_s),
        load(params_h, par_v),
        load(est_h, est_v),
        load(mixed_h, mix_v),
    ]

    barrier = pltpu.get_barrier_semaphore()
    for step in range(1, shards):
        pl.semaphore_signal(
            barrier, inc=1, device_id=(silo, lax.rem(shard + step, shards)), device_id_type=MESH
        )
    for other in (lower, upper):
        pl.semaphore_signal(barrier, inc=1, device_id=(other, shard), device_id_type=MESH)

    load_cot.wait()
    cot_t[...] = cot_v[...].T
    for copy in load_mem:
        copy.wait()
    for c in range(tiles):
        load_act[c].wait()
        grad = (
            jnp.dot(
                cot_t[...], act_v[:, pl.ds(c * block, block)], preferred_element_type=jnp.float32
            )
            * scale
        )
        for h in range(halves):
            view = pl.ds(c, total_rows, stride=tiles)
            pend[h, view, :] = pend[h, view, :] + grad[:, h * LANES : (h + 1) * LANES]

    load_kept_s.wait()
    pl.semaphore_wait(barrier, shards + 1)

    def gather(owner):
        def take(k, carry):
            row = owner * own + kept_s[owner, k]
            for h in range(halves):
                slots[owner, h, pl.ds(k, 1), :] = pend[h, pl.ds(row, 1), :]
            return carry

        lax.fori_loop(0, cap, take, 0, unroll=8)

    sends = []
    for step in list(range(1, shards)) + [0]:
        owner = lax.rem(shard + step, shards)
        gather(owner)
        if step:
            copy = remote(
                slots.at[owner], arrived.at[shard], send_sem.at[step], recv_sem.at[step],
                (silo, owner),
            )
            copy.start()
            sends.append(copy)
        else:
            arrived[shard] = slots[shard]

    for copy in load_rest:
        copy.wait()

    lane_cap = lax.broadcasted_iota(jnp.int32, (1, cap), 1)
    lane_gk = lax.broadcasted_iota(jnp.int32, (1, gk), 1)

    order = lax.broadcasted_iota(jnp.int32, (own, 1), 0)
    block_of = lax.rem(order, rows) * tiles + lax.div(order, rows)
    for pair in range(shards // 2):
        ids = []
        for source in (2 * pair, 2 * pair + 1):
            filled = lane_cap < kcnt_s[source, shard]
            ids.append(jnp.where(filled, kept_v[source, pl.ds(shard, 1), :], -1))
        ids = jnp.concatenate(ids, axis=1)
        onehot[:, pl.ds(pair * 2 * cap, 2 * cap)] = jnp.where(block_of == ids, 1.0, 0.0).astype(
            jnp.bfloat16
        )

    def gossip_hot(which):
        ids = jnp.where(lane_gk < gcnt_s[0, which], gos_v[which], -1)
        return jnp.where(block_of == ids, 1.0, 0.0)

    mine = gossip_hot(silo)
    ones = jnp.ones((gk, LANES), jnp.bfloat16)
    mask_own[...] = jnp.dot(mine.astype(jnp.bfloat16), ones, preferred_element_type=jnp.float32)
    gos_take[...] = mine.T.astype(jnp.bfloat16)
    gos_put[:, pl.ds(0, gk)] = gossip_hot(lower).astype(jnp.bfloat16)
    gos_put[:, pl.ds(gk, gk)] = gossip_hot(upper).astype(jnp.bfloat16)

    ones_cap = jnp.ones((cap, LANES), jnp.bfloat16)
    place = lax.broadcasted_iota(jnp.int32, (own, 1), 0)

    def clear(owner, carry):
        ids = jnp.where(
            lane_cap < kcnt_s[shard, owner], kept_v[shard, pl.ds(owner, 1), :], -1
        )
        hit = jnp.where(place == ids, 1.0, 0.0).astype(jnp.bfloat16)
        kept = jnp.dot(hit, ones_cap, preferred_element_type=jnp.float32)
        base = pl.multiple_of(owner * own, 8)
        for h in range(halves):
            error_o[pl.ds(base, own), pl.ds(h * LANES, LANES)] = jnp.where(
                kept > 0.0, 0.0, pend[h, pl.ds(base, own), :]
            )
        return carry

    lax.fori_loop(0, shards, clear, 0)

    for copy in sends:
        copy.wait()

    slot_rows = shards * cap
    for h in range(halves):
        high, low = split_pair(arrived[:, h].reshape(slot_rows, LANES))
        pieces[:, pl.ds(h * LANES, LANES)] = high
        pieces[:, pl.ds(block + h * LANES, LANES)] = low
    for c in range(tiles):
        part = pl.ds(c * rows, rows)
        cols = pl.ds(c * block, block)
        added = jnp.dot(onehot[part, :], pieces[...], preferred_element_type=jnp.float32)
        half = par_v[:, cols] - LEARN_RATE * (added[:, :block] + added[:, block:])
        drift = half - est_v[:, cols]
        high, low = split_pair(drift)
        drift_p[part, pl.ds(0, block)] = high
        drift_p[part, pl.ds(block, block)] = low
        mask = mask_own[part, :] > 0.0
        delta = jnp.where(jnp.concatenate([mask] * halves, axis=1), drift, 0.0)
        estimate = est_v[:, cols] + delta
        est_o[:, cols] = estimate
        mix_v[:, cols] = mix_v[:, cols] + MIX_WEIGHT * delta
        par_v[:, cols] = half - CONSENSUS * estimate

    taken = jnp.dot(gos_take[...], drift_p[...], preferred_element_type=jnp.float32)
    gos_send[...] = taken[:, :block] + taken[:, block:]
    goes = [
        remote(gos_send, gos_recv.at[0], gsend_sem.at[0], grecv_sem.at[0], (upper, shard)),
        remote(gos_send, gos_recv.at[1], gsend_sem.at[1], grecv_sem.at[1], (lower, shard)),
    ]
    for copy in goes:
        copy.start()
    for copy in goes:
        copy.wait()
    high, low = split_pair(gos_recv[...].reshape(2 * gk, block))
    gos_p[:, pl.ds(0, block)] = high
    gos_p[:, pl.ds(block, block)] = low
    for c in range(tiles):
        cols = pl.ds(c * block, block)
        near = jnp.dot(
            gos_put[pl.ds(c * rows, rows), :], gos_p[...], preferred_element_type=jnp.float32
        )
        mixed = mix_v[:, cols] + MIX_WEIGHT * (near[:, :block] + near[:, block:])
        mixed_o[:, cols] = mixed
        params_o[:, cols] = par_v[:, cols] + CONSENSUS * mixed


def body(
    activ, cotangent, error_memory, params, estimate, mixed,
    kept_blocks, kept_counts, gossip_blocks, gossip_counts,
):
    silos, shards = lax.axis_size("silo"), lax.axis_size("shard")
    tokens, width_in = activ.shape
    width_out = cotangent.shape[1]
    nblocks, block = error_memory.shape[2:]
    own = nblocks // shards
    cap, gk = kept_blocks.shape[3], gossip_blocks.shape[2]
    tiles = width_in // block
    halves = block // LANES
    rows = own // tiles
    f32, bf16, i32 = jnp.float32, jnp.bfloat16, jnp.int32
    dims = (silos, shards, own, cap, gk, tiles, block)
    operands = (
        activ, cotangent, error_memory[0, 0], params[0], estimate[0], mixed[0],
        kept_blocks[0], kept_counts[0], gossip_blocks, gossip_counts.reshape(1, silos),
    )
    operands = tuple(pltpu.with_memory_space_constraint(x, pltpu.HBM) for x in operands)
    vmem = pltpu.VMEM
    outs = pl.pallas_call(
        functools.partial(kernel, dims),
        out_shape=(
            vmem((rows, width_in), f32),
            vmem((rows, width_in), f32),
            vmem((rows, width_in), f32),
            vmem((nblocks, block), f32),
        ),
        in_specs=[pl.BlockSpec(memory_space=pltpu.HBM)] * len(operands),
        out_specs=tuple([pl.BlockSpec(memory_space=pltpu.VMEM)] * 4),
        scratch_shapes=[
            vmem((tokens, width_in), bf16),
            vmem((tokens, width_out), bf16),
            vmem((width_out, tokens), bf16),
            vmem((halves, nblocks, LANES), f32),
            vmem((shards, halves, cap, LANES), f32),
            vmem((shards, halves, cap, LANES), f32),
            vmem((shards * cap, 2 * block), bf16),
            vmem((own, shards * cap), bf16),
            vmem((own, LANES), f32),
            vmem((gk, own), bf16),
            vmem((own, 2 * gk), bf16),
            vmem((own, 2 * block), bf16),
            vmem((gk, block), f32),
            vmem((2, gk, block), f32),
            vmem((2 * gk, 2 * block), bf16),
            vmem((rows, width_in), f32),
            vmem((rows, width_in), f32),
            vmem((rows, width_in), f32),
            vmem((shards, shards, cap), i32),
            vmem((silos, 1, gk), i32),
            pltpu.SMEM((shards, cap), i32),
            pltpu.SMEM((shards, shards), i32),
            pltpu.SMEM((1, silos), i32),
            pltpu.SemaphoreType.DMA((16,)),
            pltpu.SemaphoreType.DMA((shards,)),
            pltpu.SemaphoreType.DMA((shards,)),
            pltpu.SemaphoreType.DMA((2,)),
            pltpu.SemaphoreType.DMA((2,)),
        ],
        compiler_params=pltpu.CompilerParams(
            collective_id=0, has_side_effects=True, vmem_limit_bytes=24 << 20
        ),
    )(*operands)
    return (
        outs[0].reshape(params.shape),
        outs[1].reshape(estimate.shape),
        outs[2].reshape(mixed.shape),
        outs[3].reshape(error_memory.shape),
    )


def solution(mesh):
    in_specs = (
        P(("silo", "shard"), None),
        P(("silo", "shard"), None),
        P("silo", "shard", None, None),
        P("silo", "shard", None),
        P("silo", "shard", None),
        P("silo", "shard", None),
        P("silo", None, None, None),
        P("silo", None, None),
        P(None, "shard", None),
        P(None, "shard"),
    )
    out_specs = (
        P("silo", "shard", None),
        P("silo", "shard", None),
        P("silo", "shard", None),
        P("silo", "shard", None, None),
    )
    return jax.shard_map(body, mesh=mesh, in_specs=in_specs, out_specs=out_specs, check_vma=False)
```

time: 75.1 us -> 31.7 us (0.42)
  the two profiles are of different devices: /device:TPU:17 before, /device:TPU:16 now
where the time goes in v1:
time: 31.7 us
  Pallas kernels  27 us (85%)
  local copies, waits for them, and re-layouts  3.96 us (12%)
  between operations  0.64 us (2%)
    pallas_call x1, Pallas kernels, body(): pl.pallas_call(functools.partial(kernel, dims), out_shape=(vmem((rows, wi...  27 us
    unnamed x4, local copies, waits for them, and re-layouts  3.96 us

profile of v1, /device:TPU:16, one launch (start us, length us, event | category | flops | bytes accessed | tf_op | source)
XLA Modules:
  0.0 31.7 jit_solution(11626396375828380513)
XLA Ops:
  0.6 27.0 %shard_map.129 = (f32[80,1280]{1,0:T(8,128)S(1)}, f32[80,1280]{1,0:T(8,128)S(1)}, f32[80,1280]{1,0:T(8,128)S(1)}, f32[3200,256]{1,0:T(8,128)S(1)}) custom-call(bf16[1024,1280]{1,0:T(8,128)(2,1)} %activ_h.1, bf16[1024,640]{1,0:T(8,128)(2,1)} %cot_h.1, f32[3200,256]{1,0:T(8,128)} %bitcast.15, f32[80,1280]{1,0:T(8,128)} %bitcast.16, f32[80,1280]{1,0:T(8,128)} %bitcast.17, ...), custom_call_target="tpu_custom_call" | custom-call | tf_op jit(solution)/shard_map/pallas_call | solution.py:239
  27.7 0.8 %copy.18 = f32[1,80,1280]{2,1,0:T(8,128)} copy(f32[1,80,1280]{2,1,0:T(8,128)S(1)} %bitcast.14) | data formatting | bytes 819200
  28.4 0.8 %copy.19 = f32[1,80,1280]{2,1,0:T(8,128)} copy(f32[1,80,1280]{2,1,0:T(8,128)S(1)} %bitcast.13) | data formatting | bytes 819200
  29.2 0.8 %copy.20 = f32[1,80,1280]{2,1,0:T(8,128)} copy(f32[1,80,1280]{2,1,0:T(8,128)S(1)} %bitcast.12) | data formatting | bytes 819200
  29.9 1.7 %copy.21 = f32[1,1,3200,256]{3,2,1,0:T(8,128)} copy(f32[1,1,3200,256]{3,2,1,0:T(8,128)S(1)} %bitcast.11) | data formatting | bytes 6553600

commit v2 on v1

v2 whole, which is shorter than its diff:
```python
import functools

import jax
import jax.numpy as jnp
from jax import lax
from jax.experimental import pallas as pl
from jax.experimental.pallas import tpu as pltpu
from jax.sharding import PartitionSpec as P

LEARN_RATE = 0.25
CONSENSUS = 0.5
MIX_WEIGHT = 1.0 / 3.0
MESH = pl.DeviceIdType.MESH
LANES = 128


def split_pair(value):
    high = value.astype(jnp.bfloat16)
    low = (value - high.astype(jnp.float32)).astype(jnp.bfloat16)
    return high, low


def remote(src, dst, send, recv, target):
    return pltpu.make_async_remote_copy(
        src_ref=src, dst_ref=dst, send_sem=send, recv_sem=recv,
        device_id=target, device_id_type=MESH,
    )


def kernel(
    dims,
    activ_h, cot_h, mem_h, params_h, est_h, mixed_h, kept_h, kcnt_h, gos_h, gcnt_h,
    params_o, est_o, mixed_o, error_o,
    act_a, act_b, cot_v, cot_t, pend_a, pend_b, slots, arrived, pieces, onehot, mask_own, gos_take, gos_put,
    drift_p, gos_send, gos_recv, gos_p, par_v, est_v, mix_v, kept_v, gos_v,
    kept_s, kcnt_s, gcnt_s,
    load_sem, send_sem, recv_sem, gsend_sem, grecv_sem,
):
    silos, shards, own, cap, gk, tiles, block = dims
    rows = own // tiles
    act_v, pend = (act_a, act_b), (pend_a, pend_b)
    halves = len(pend)
    all_rows = rows * shards
    silo = lax.axis_index("silo")
    shard = lax.axis_index("shard")
    upper = lax.rem(silo + 1, silos)
    lower = lax.rem(silo + silos - 1, silos)
    scale = float(activ_h.shape[1]) ** -0.5
    count = [0]

    def load(src, dst):
        copy = pltpu.make_async_copy(src, dst, load_sem.at[count[0]])
        count[0] += 1
        copy.start()
        return copy

    def lanes_of(c, h):
        return pl.ds(c * block + h * LANES, LANES)

    def load_half(h):
        return [
            load(activ_h.at[:, lanes_of(c, h)], act_v[h].at[:, pl.ds(c * LANES, LANES)])
            for c in range(tiles)
        ]

    load_cot = load(cot_h, cot_v)
    load_kept_s = load(kept_h.at[shard], kept_s)
    load_act = [load_half(0)]

    barrier = pltpu.get_barrier_semaphore()
    for step in range(1, shards):
        pl.semaphore_signal(
            barrier, inc=1, device_id=(silo, lax.rem(shard + step, shards)), device_id_type=MESH
        )
    for other in (lower, upper):
        pl.semaphore_signal(barrier, inc=1, device_id=(other, shard), device_id_type=MESH)

    load_cot.wait()
    load_mem = []
    for h in range(halves):
        load_mem.append(load(mem_h.at[:, pl.ds(h * LANES, LANES)], pend[h]))
        if h + 1 < halves:
            load_act.append(load_half(h + 1))
    load_rest = [
        load(kept_h, kept_v),
        load(kcnt_h, kcnt_s),
        load(gos_h, gos_v),
        load(gcnt_h, gcnt_s),
        load(params_h, par_v),
        load(est_h, est_v),
        load(mixed_h, mix_v),
    ]
    cot_t[...] = cot_v[...].T

    def multiply(h):
        for copy in load_act[h]:
            copy.wait()
        for first in range(0, tiles, 2):
            these = range(first, min(first + 2, tiles))
            right = act_v[h][:, pl.ds(first * LANES, len(these) * LANES)]
            grad = jnp.dot(cot_t[...], right, preferred_element_type=jnp.float32) * scale
            if first == 0:
                load_mem[h].wait()
            for j, c in enumerate(these):
                view = pl.ds(c, all_rows, stride=tiles)
                pend[h][view, :] = pend[h][view, :] + grad[:, j * LANES : (j + 1) * LANES]

    def gather(owner, h):
        base = pl.multiple_of(owner * own, 8)

        def take(step, carry):
            first = pl.multiple_of(step * 8, 8)
            for j in range(8):
                row = base + kept_s[owner, first + j]
                slots[h, owner, pl.ds(first + j, 1), :] = pend[h][pl.ds(row, 1), :]
            return carry

        lax.fori_loop(0, cap // 8, take, 0)

    pairs = shards // 2
    sends = []
    for h in range(halves):
        multiply(h)
        if h == 0:
            load_kept_s.wait()
        if h == 0:
            pl.semaphore_wait(barrier, shards + 1)
        sends.append([])
        for far, side in ((2, 1), (1, 0), (3, 0), (1, 1), (3, 1), (2, 0), (0, 1), (0, 0)):
            owner = 2 * lax.rem(lax.div(shard, 2) + far, pairs) + lax.rem(shard + side, 2)
            gather(owner, h)
            step = 2 * far + side
            if step:
                copy = remote(
                    slots.at[h, owner], arrived.at[h, shard], send_sem.at[h, step],
                    recv_sem.at[h, step], (silo, owner),
                )
                copy.start()
                sends[h].append(copy)
            else:
                arrived[h, shard] = slots[h, shard]

    for copy in load_rest:
        copy.wait()

    lane_cap = lax.broadcasted_iota(jnp.int32, (1, cap), 1)
    lane_gk = lax.broadcasted_iota(jnp.int32, (1, gk), 1)

    order = lax.broadcasted_iota(jnp.int32, (own, 1), 0)
    block_of = lax.rem(order, rows) * tiles + lax.div(order, rows)
    for pair in range(shards // 2):
        ids = []
        for source in (2 * pair, 2 * pair + 1):
            filled = lane_cap < kcnt_s[source, shard]
            ids.append(jnp.where(filled, kept_v[source, pl.ds(shard, 1), :], -1))
        ids = jnp.concatenate(ids, axis=1)
        onehot[:, pl.ds(pair * 2 * cap, 2 * cap)] = jnp.where(block_of == ids, 1.0, 0.0).astype(
            jnp.bfloat16
        )

    def gossip_hot(which):
        ids = jnp.where(lane_gk < gcnt_s[0, which], gos_v[which], -1)
        return jnp.where(block_of == ids, 1.0, 0.0)

    mine = gossip_hot(silo)
    ones = jnp.ones((gk, LANES), jnp.bfloat16)
    mask_own[...] = jnp.dot(mine.astype(jnp.bfloat16), ones, preferred_element_type=jnp.float32)
    gos_take[...] = mine.T.astype(jnp.bfloat16)
    gos_put[:, pl.ds(0, gk)] = gossip_hot(lower).astype(jnp.bfloat16)
    gos_put[:, pl.ds(gk, gk)] = gossip_hot(upper).astype(jnp.bfloat16)

    goes = []

    def settle(h):
        for copy in sends[h]:
            copy.wait_recv()
        high, low = split_pair(arrived[h].reshape(shards * cap, LANES))
        pieces[h, :, pl.ds(0, LANES)] = high
        pieces[h, :, pl.ds(LANES, LANES)] = low
        added = jnp.dot(onehot[...], pieces[h], preferred_element_type=jnp.float32)
        added = added[:, :LANES] + added[:, LANES:]
        for c in range(tiles):
            part = pl.ds(c * rows, rows)
            cols = lanes_of(c, h)
            half = par_v[:, cols] - LEARN_RATE * added[c * rows : (c + 1) * rows]
            drift = half - est_v[:, cols]
            high, low = split_pair(drift)
            drift_p[h, part, pl.ds(0, LANES)] = high
            drift_p[h, part, pl.ds(LANES, LANES)] = low
            delta = jnp.where(mask_own[part, :] > 0.0, drift, 0.0)
            estimate = est_v[:, cols] + delta
            est_o[:, cols] = estimate
            mix_v[:, cols] = mix_v[:, cols] + MIX_WEIGHT * delta
            par_v[:, cols] = half - CONSENSUS * estimate
        taken = jnp.dot(gos_take[...], drift_p[h], preferred_element_type=jnp.float32)
        gos_send[h] = taken[:, :LANES] + taken[:, LANES:]
        for place, target in ((0, upper), (1, lower)):
            copy = remote(
                gos_send.at[h], gos_recv.at[h, place], gsend_sem.at[h, place],
                grecv_sem.at[h, place], (target, shard),
            )
            copy.start()
            goes.append(copy)

    def close(h):
        for copy in goes[2 * h : 2 * h + 2]:
            copy.wait_recv()
        high, low = split_pair(gos_recv[h].reshape(2 * gk, LANES))
        gos_p[h, :, pl.ds(0, LANES)] = high
        gos_p[h, :, pl.ds(LANES, LANES)] = low
        near = jnp.dot(gos_put[...], gos_p[h], preferred_element_type=jnp.float32)
        near = near[:, :LANES] + near[:, LANES:]
        for c in range(tiles):
            cols = lanes_of(c, h)
            mixed = mix_v[:, cols] + MIX_WEIGHT * near[c * rows : (c + 1) * rows]
            mixed_o[:, cols] = mixed
            params_o[:, cols] = par_v[:, cols] + CONSENSUS * mixed

    ones_cap = jnp.ones((cap, LANES), jnp.bfloat16)
    place_of = lax.broadcasted_iota(jnp.int32, (own, 1), 0)

    def clear(owner, carry):
        ids = jnp.where(lane_cap < kcnt_s[shard, owner], kept_v[shard, pl.ds(owner, 1), :], -1)
        hit = jnp.where(place_of == ids, 1.0, 0.0).astype(jnp.bfloat16)
        kept = jnp.dot(hit, ones_cap, preferred_element_type=jnp.float32)
        base = pl.multiple_of(owner * own, 8)
        for h in range(halves):
            error_o[pl.ds(base, own), pl.ds(h * LANES, LANES)] = jnp.where(
                kept > 0.0, 0.0, pend[h][pl.ds(base, own), :]
            )
        return carry

    settle(0)
    lax.fori_loop(0, shards, clear, 0)
    for h in range(1, halves):
        settle(h)
    for h in range(halves):
        close(h)
    for copy in [copy for group in sends for copy in group] + goes:
        copy.wait_send()


def finish(*refs):
    count = len(refs) // 2
    sems = refs[-1]
    copies = [
        pltpu.make_async_copy(refs[i], refs[count + i], sems.at[i]) for i in range(count)
    ]
    for copy in copies:
        copy.start()
    for copy in copies:
        copy.wait()


def body(
    activ, cotangent, error_memory, params, estimate, mixed,
    kept_blocks, kept_counts, gossip_blocks, gossip_counts,
):
    silos, shards = lax.axis_size("silo"), lax.axis_size("shard")
    tokens, width_in = activ.shape
    width_out = cotangent.shape[1]
    nblocks, block = error_memory.shape[2:]
    own = nblocks // shards
    cap, gk = kept_blocks.shape[3], gossip_blocks.shape[2]
    tiles = width_in // block
    halves = 2
    assert block == halves * LANES
    rows = own // tiles
    f32, bf16, i32 = jnp.float32, jnp.bfloat16, jnp.int32
    dims = (silos, shards, own, cap, gk, tiles, block)
    operands = (
        activ, cotangent, error_memory[0, 0], params[0], estimate[0], mixed[0],
        kept_blocks[0], kept_counts[0], gossip_blocks, gossip_counts.reshape(1, silos),
    )
    operands = tuple(pltpu.with_memory_space_constraint(x, pltpu.HBM) for x in operands)
    vmem = pltpu.VMEM
    outs = pl.pallas_call(
        functools.partial(kernel, dims),
        out_shape=(
            vmem((rows, width_in), f32),
            vmem((rows, width_in), f32),
            vmem((rows, width_in), f32),
            vmem((nblocks, block), f32),
        ),
        in_specs=[pl.BlockSpec(memory_space=pltpu.HBM)] * len(operands),
        out_specs=tuple([pl.BlockSpec(memory_space=pltpu.VMEM)] * 4),
        scratch_shapes=[
            vmem((tokens, tiles * LANES), bf16),
            vmem((tokens, tiles * LANES), bf16),
            vmem((tokens, width_out), bf16),
            vmem((width_out, tokens), bf16),
            vmem((nblocks, LANES), f32),
            vmem((nblocks, LANES), f32),
            vmem((halves, shards, cap, LANES), f32),
            vmem((halves, shards, cap, LANES), f32),
            vmem((halves, shards * cap, 2 * LANES), bf16),
            vmem((own, shards * cap), bf16),
            vmem((own, LANES), f32),
            vmem((gk, own), bf16),
            vmem((own, 2 * gk), bf16),
            vmem((halves, own, 2 * LANES), bf16),
            vmem((halves, gk, LANES), f32),
            vmem((halves, 2, gk, LANES), f32),
            vmem((halves, 2 * gk, 2 * LANES), bf16),
            vmem((rows, width_in), f32),
            vmem((rows, width_in), f32),
            vmem((rows, width_in), f32),
            vmem((shards, shards, cap), i32),
            vmem((silos, 1, gk), i32),
            pltpu.SMEM((shards, cap), i32),
            pltpu.SMEM((shards, shards), i32),
            pltpu.SMEM((1, silos), i32),
            pltpu.SemaphoreType.DMA((2 + halves * (tiles + 1) + 7,)),
            pltpu.SemaphoreType.DMA((halves, shards)),
            pltpu.SemaphoreType.DMA((halves, shards)),
            pltpu.SemaphoreType.DMA((halves, 2)),
            pltpu.SemaphoreType.DMA((halves, 2)),
        ],
        compiler_params=pltpu.CompilerParams(
            collective_id=0, has_side_effects=True, vmem_limit_bytes=24 << 20
        ),
    )(*operands)
    outs = pl.pallas_call(
        finish,
        out_shape=tuple(jax.ShapeDtypeStruct(x.shape, x.dtype) for x in outs),
        in_specs=[pl.BlockSpec(memory_space=pltpu.VMEM)] * len(outs),
        out_specs=tuple([pl.BlockSpec(memory_space=pltpu.HBM)] * len(outs)),
        scratch_shapes=[pltpu.SemaphoreType.DMA((len(outs),))],
        compiler_params=pltpu.CompilerParams(vmem_limit_bytes=1 << 20),
    )(*outs)
    return (
        outs[0].reshape(params.shape),
        outs[1].reshape(estimate.shape),
        outs[2].reshape(mixed.shape),
        outs[3].reshape(error_memory.shape),
    )


def solution(mesh):
    in_specs = (
        P(("silo", "shard"), None),
        P(("silo", "shard"), None),
        P("silo", "shard", None, None),
        P("silo", "shard", None),
        P("silo", "shard", None),
        P("silo", "shard", None),
        P("silo", None, None, None),
        P("silo", None, None),
        P(None, "shard", None),
        P(None, "shard"),
    )
    out_specs = (
        P("silo", "shard", None),
        P("silo", "shard", None),
        P("silo", "shard", None),
        P("silo", "shard", None, None),
    )
    return jax.shard_map(body, mesh=mesh, in_specs=in_specs, out_specs=out_specs, check_vma=False)
```

time: 31.7 us -> 27.4 us (0.86)
  the two profiles are of different devices: /device:TPU:16 before, /device:TPU:6 now
where the time goes in v2:
time: 27.4 us; the launch traced here: 27.3 us
  Pallas kernels  26.7 us (97%)
  between operations  0.64 us (2%)
    pallas_call x1, Pallas kernels, body(): pl.pallas_call(functools.partial(kernel, dims), out_shape=(vmem((rows, wi...  24.5 us
    pallas_call x1, Pallas kernels, body(): pl.pallas_call(finish, out_shape=tuple((jax.ShapeDtypeStruct(x.shape, x.d...  2.15 us

profile of v2, /device:TPU:6, one launch (start us, length us, event | category | flops | bytes accessed | tf_op | source)
XLA Modules:
  0.0 27.3 jit_solution(11394909053147478801)
XLA Ops:
  0.6 24.5 %shard_map.129 = (f32[80,1280]{1,0:T(8,128)S(1)}, f32[80,1280]{1,0:T(8,128)S(1)}, f32[80,1280]{1,0:T(8,128)S(1)}, f32[3200,256]{1,0:T(8,128)S(1)}) custom-call(bf16[1024,1280]{1,0:T(8,128)(2,1)} %activ_h.1, bf16[1024,640]{1,0:T(8,128)(2,1)} %cot_h.1, f32[3200,256]{1,0:T(8,128)} %bitcast.11, f32[80,1280]{1,0:T(8,128)} %bitcast.12, f32[80,1280]{1,0:T(8,128)} %bitcast.13, ...), custom_call_target="tpu_custom_call" | custom-call | tf_op jit(solution)/shard_map/pallas_call | solution.py:277
  25.2 2.2 %shard_map.130 = (f32[80,1280]{1,0:T(8,128)}, f32[80,1280]{1,0:T(8,128)}, f32[80,1280]{1,0:T(8,128)}, f32[3200,256]{1,0:T(8,128)}) custom-call(f32[80,1280]{1,0:T(8,128)S(1)} %get-tuple-element.12.refs_0_, f32[80,1280]{1,0:T(8,128)S(1)} %get-tuple-element.13.refs_1_, f32[80,1280]{1,0:T(8,128)S(1)} %get-tuple-element.14.refs_2_, ...), custom_call_target="tpu_custom_call" | custom-call | tf_op jit(solution)/shard_map/pallas_call | solution.py:323

commit v3 on v2

--- a/solution.py
+++ b/solution.py
@@ -31,7 +31,7 @@
     dims,
     activ_h, cot_h, mem_h, params_h, est_h, mixed_h, kept_h, kcnt_h, gos_h, gcnt_h,
     params_o, est_o, mixed_o, error_o,
-    act_a, act_b, cot_v, cot_t, pend_a, pend_b, slots, arrived, pieces, onehot, mask_own, gos_take, gos_put,
+    act_a, act_b, cot_v, cot_t, pend_a, pend_b, slots, arrived, pieces, onehot, mask_own, gos_take, gos_put, gos_mix, gos_base,
     drift_p, gos_send, gos_recv, gos_p, par_v, est_v, mix_v, kept_v, gos_v,
     kept_s, kcnt_s, gcnt_s,
     load_sem, send_sem, recv_sem, gsend_sem, grecv_sem,
@@ -64,8 +64,9 @@
         ]
 
     load_cot = load(cot_h, cot_v)
+    load_act = [load_half(0)]
     load_kept_s = load(kept_h.at[shard], kept_s)
-    load_act = [load_half(0)]
+    load_mem = [load(mem_h.at[:, pl.ds(0, LANES)], pend[0])]
 
     barrier = pltpu.get_barrier_semaphore()
     for step in range(1, shards):
@@ -76,21 +77,23 @@
         pl.semaphore_signal(barrier, inc=1, device_id=(other, shard), device_id_type=MESH)
 
     load_cot.wait()
-    load_mem = []
-    for h in range(halves):
-        load_mem.append(load(mem_h.at[:, pl.ds(h * LANES, LANES)], pend[h]))
-        if h + 1 < halves:
-            load_act.append(load_half(h + 1))
-    load_rest = [
-        load(kept_h, kept_v),
-        load(kcnt_h, kcnt_s),
-        load(gos_h, gos_v),
-        load(gcnt_h, gcnt_s),
-        load(params_h, par_v),
-        load(est_h, est_v),
-        load(mixed_h, mix_v),
-    ]
     cot_t[...] = cot_v[...].T
+
+    late = []
+
+    def later():
+        for h in range(1, halves):
+            load_act.append(load_half(h))
+            load_mem.append(load(mem_h.at[:, pl.ds(h * LANES, LANES)], pend[h]))
+        return [
+            load(kept_h, kept_v),
+            load(kcnt_h, kcnt_s),
+            load(gos_h, gos_v),
+            load(gcnt_h, gcnt_s),
+            load(params_h, par_v),
+            load(est_h, est_v),
+            load(mixed_h, mix_v),
+        ]
 
     def multiply(h):
         for copy in load_act[h]:
@@ -101,21 +104,16 @@
             grad = jnp.dot(cot_t[...], right, preferred_element_type=jnp.float32) * scale
             if first == 0:
                 load_mem[h].wait()
+                if h == 0:
+                    late.extend(later())
             for j, c in enumerate(these):
                 view = pl.ds(c, all_rows, stride=tiles)
                 pend[h][view, :] = pend[h][view, :] + grad[:, j * LANES : (j + 1) * LANES]
 
     def gather(owner, h):
-        base = pl.multiple_of(owner * own, 8)
-
-        def take(step, carry):
-            first = pl.multiple_of(step * 8, 8)
-            for j in range(8):
-                row = base + kept_s[owner, first + j]
-                slots[h, owner, pl.ds(first + j, 1), :] = pend[h][pl.ds(row, 1), :]
-            return carry
-
-        lax.fori_loop(0, cap // 8, take, 0)
+        blocks = pend[h].at[pl.ds(pl.multiple_of(owner * own, 8), own)]
+        for k in range(cap):
+            slots[h, owner, pl.ds(k, 1), :] = blocks[pl.ds(kept_s[owner, k], 1), :]
 
     pairs = shards // 2
     sends = []
@@ -140,7 +138,7 @@
             else:
                 arrived[h, shard] = slots[h, shard]
 
-    for copy in load_rest:
+    for copy in late:
         copy.wait()
 
     lane_cap = lax.broadcasted_iota(jnp.int32, (1, cap), 1)
@@ -169,6 +167,18 @@
     gos_put[:, pl.ds(0, gk)] = gossip_hot(lower).astype(jnp.bfloat16)
     gos_put[:, pl.ds(gk, gk)] = gossip_hot(upper).astype(jnp.bfloat16)
 
+    gos_mix[...] = jnp.dot(
+        gos_take[...], onehot[...], preferred_element_type=jnp.float32
+    ).astype(jnp.bfloat16)
+    for h in range(halves):
+        for c in range(tiles):
+            part = pl.ds(c * rows, rows)
+            high, low = split_pair(par_v[:, lanes_of(c, h)] - est_v[:, lanes_of(c, h)])
+            drift_p[part, pl.ds(0, LANES)] = high
+            drift_p[part, pl.ds(LANES, LANES)] = low
+        taken = jnp.dot(gos_take[...], drift_p[...], preferred_element_type=jnp.float32)
+        gos_base[h] = taken[:, :LANES] + taken[:, LANES:]
+
     goes = []
 
     def settle(h):
@@ -177,23 +187,8 @@
         high, low = split_pair(arrived[h].reshape(shards * cap, LANES))
         pieces[h, :, pl.ds(0, LANES)] = high
         pieces[h, :, pl.ds(LANES, LANES)] = low
-        added = jnp.dot(onehot[...], pieces[h], preferred_element_type=jnp.float32)
-        added = added[:, :LANES] + added[:, LANES:]
-        for c in range(tiles):
-            part = pl.ds(c * rows, rows)
-            cols = lanes_of(c, h)
-            half = par_v[:, cols] - LEARN_RATE * added[c * rows : (c + 1) * rows]
-            drift = half - est_v[:, cols]
-            high, low = split_pair(drift)
-            drift_p[h, part, pl.ds(0, LANES)] = high
-            drift_p[h, part, pl.ds(LANES, LANES)] = low
-            delta = jnp.where(mask_own[part, :] > 0.0, drift, 0.0)
-            estimate = est_v[:, cols] + delta
-            est_o[:, cols] = estimate
-            mix_v[:, cols] = mix_v[:, cols] + MIX_WEIGHT * delta
-            par_v[:, cols] = half - CONSENSUS * estimate
-        taken = jnp.dot(gos_take[...], drift_p[h], preferred_element_type=jnp.float32)
-        gos_send[h] = taken[:, :LANES] + taken[:, LANES:]
+        taken = jnp.dot(gos_mix[...], pieces[h], preferred_element_type=jnp.float32)
+        gos_send[h] = gos_base[h] - LEARN_RATE * (taken[:, :LANES] + taken[:, LANES:])
         for place, target in ((0, upper), (1, lower)):
             copy = remote(
                 gos_send.at[h], gos_recv.at[h, place], gsend_sem.at[h, place],
@@ -201,6 +196,19 @@
             )
             copy.start()
             goes.append(copy)
+
+    def update(h):
+        added = jnp.dot(onehot[...], pieces[h], preferred_element_type=jnp.float32)
+        added = added[:, :LANES] + added[:, LANES:]
+        for c in range(tiles):
+            part = pl.ds(c * rows, rows)
+            cols = lanes_of(c, h)
+            half = par_v[:, cols] - LEARN_RATE * added[c * rows : (c + 1) * rows]
+            delta = jnp.where(mask_own[part, :] > 0.0, half - est_v[:, cols], 0.0)
+            estimate = est_v[:, cols] + delta
+            est_o[:, cols] = estimate
+            mix_v[:, cols] = mix_v[:, cols] + MIX_WEIGHT * delta
+            par_v[:, cols] = half - CONSENSUS * estimate
 
     def close(h):
         for copy in goes[2 * h : 2 * h + 2]:
@@ -230,10 +238,10 @@
             )
         return carry
 
-    settle(0)
     lax.fori_loop(0, shards, clear, 0)
-    for h in range(1, halves):
+    for h in range(halves):
         settle(h)
+        update(h)
     for h in range(halves):
         close(h)
     for copy in [copy for group in sends for copy in group] + goes:
@@ -298,7 +306,9 @@
             vmem((own, LANES), f32),
             vmem((gk, own), bf16),
             vmem((own, 2 * gk), bf16),
-            vmem((halves, own, 2 * LANES), bf16),
+            vmem((gk, shards * cap), bf16),
+            vmem((halves, gk, LANES), f32),
+            vmem((own, 2 * LANES), bf16),
             vmem((halves, gk, LANES), f32),
             vmem((halves, 2, gk, LANES), f32),
             vmem((halves, 2 * gk, 2 * LANES), bf16),

time: 27.4 us -> 25.5 us (0.931)
  Pallas kernels: 26.7 us -> 24.7 us
    pallas_call x1, Pallas kernels: 24.5 us -> 22.6 us  [body(): pl.pallas_call(functools.partial(kernel, dims), out_shape=(vmem((rows, wi...]
where the time goes in v3:
time: 25.5 us; the launch traced here: 25.4 us
  Pallas kernels  24.7 us (97%)
  between operations  0.64 us (3%)
    pallas_call x1, Pallas kernels, body(): pl.pallas_call(functools.partial(kernel, dims), out_shape=(vmem((rows, wi...  22.6 us
    pallas_call x1, Pallas kernels, body(): pl.pallas_call(finish, out_shape=tuple((jax.ShapeDtypeStruct(x.shape, x.d...  2.15 us

profile of v3, /device:TPU:6, one launch (start us, length us, event | category | flops | bytes accessed | tf_op | source)
XLA Modules:
  0.0 25.4 jit_solution(5076104760732159579)
XLA Ops:
  0.6 22.6 %shard_map.129 = (f32[80,1280]{1,0:T(8,128)S(1)}, f32[80,1280]{1,0:T(8,128)S(1)}, f32[80,1280]{1,0:T(8,128)S(1)}, f32[3200,256]{1,0:T(8,128)S(1)}) custom-call(bf16[1024,1280]{1,0:T(8,128)(2,1)} %activ_h.1, bf16[1024,640]{1,0:T(8,128)(2,1)} %cot_h.1, f32[3200,256]{1,0:T(8,128)} %bitcast.11, f32[80,1280]{1,0:T(8,128)} %bitcast.12, f32[80,1280]{1,0:T(8,128)} %bitcast.13, ...), custom_call_target="tpu_custom_call" | custom-call | tf_op jit(solution)/shard_map/pallas_call | solution.py:285
  23.2 2.2 %shard_map.130 = (f32[80,1280]{1,0:T(8,128)}, f32[80,1280]{1,0:T(8,128)}, f32[80,1280]{1,0:T(8,128)}, f32[3200,256]{1,0:T(8,128)}) custom-call(f32[80,1280]{1,0:T(8,128)S(1)} %get-tuple-element.12.refs_0_, f32[80,1280]{1,0:T(8,128)S(1)} %get-tuple-element.13.refs_1_, f32[80,1280]{1,0:T(8,128)S(1)} %get-tuple-element.14.refs_2_, ...), custom_call_target="tpu_custom_call" | custom-call | tf_op jit(solution)/shard_map/pallas_call | solution.py:333

commit v4 on v3

--- a/solution.py
+++ b/solution.py
@@ -34,7 +34,7 @@
     act_a, act_b, cot_v, cot_t, pend_a, pend_b, slots, arrived, pieces, onehot, mask_own, gos_take, gos_put, gos_mix, gos_base,
     drift_p, gos_send, gos_recv, gos_p, par_v, est_v, mix_v, kept_v, gos_v,
     kept_s, kcnt_s, gcnt_s,
-    load_sem, send_sem, recv_sem, gsend_sem, grecv_sem,
+    load_sem, send_sem, recv_sem, gsend_sem, grecv_sem, near_sem,
 ):
     silos, shards, own, cap, gk, tiles, block = dims
     rows = own // tiles
@@ -73,11 +73,49 @@
         pl.semaphore_signal(
             barrier, inc=1, device_id=(silo, lax.rem(shard + step, shards)), device_id_type=MESH
         )
-    for other in (lower, upper):
-        pl.semaphore_signal(barrier, inc=1, device_id=(other, shard), device_id_type=MESH)
+    last = silos - 1
+
+    @pl.when(silo != last)
+    def _():
+        pl.semaphore_signal(barrier, inc=1, device_id=(upper, shard), device_id_type=MESH)
+
+    @pl.when(silo == 0)
+    def _():
+        pl.semaphore_signal(barrier, inc=1, device_id=(lower, shard), device_id_type=MESH)
+
+    def enter():
+        greeted = jnp.where(silo == 0, 0, jnp.where(silo == last, 2, 1))
+        pl.semaphore_wait(barrier, shards - 1 + greeted)
+
+        @pl.when(silo != 0)
+        def _():
+            pl.semaphore_signal(near_sem, inc=1, device_id=(lower, shard), device_id_type=MESH)
+
+        @pl.when(silo == last)
+        def _():
+            pl.semaphore_signal(near_sem, inc=1, device_id=(upper, shard), device_id_type=MESH)
+
+    def await_near():
+        @pl.when(silo != last)
+        def _():
+            pl.semaphore_wait(near_sem, jnp.where(silo == 0, 2, 1))
 
     load_cot.wait()
-    cot_t[...] = cot_v[...].T
+    pairs = shards // 2
+    here, side = lax.div(shard, 2), lax.rem(shard, 2)
+
+    def owner_at(turn):
+        far = (turn + 1) % pairs
+        return 2 * lax.rem(here + far, pairs) + (1 - side if turn < pairs else side)
+
+    turned = cot_v[...].T
+    for owner in range(shards):
+        turn = lax.rem(owner // 2 - here + 2 * pairs - 1, pairs) + jnp.where(
+            side == owner % 2, pairs, 0
+        )
+        cot_t[pl.ds(pl.multiple_of(turn * rows, 16), rows), :] = turned[
+            owner * rows : (owner + 1) * rows
+        ]
 
     late = []
 
@@ -95,48 +133,53 @@
             load(mixed_h, mix_v),
         ]
 
-    def multiply(h):
-        for copy in load_act[h]:
-            copy.wait()
+    def multiply(h, turns):
+        if turns[0] == 0:
+            for copy in load_act[h]:
+                copy.wait()
+        left = cot_t[turns[0] * rows : (turns[-1] + 1) * rows, :]
         for first in range(0, tiles, 2):
             these = range(first, min(first + 2, tiles))
             right = act_v[h][:, pl.ds(first * LANES, len(these) * LANES)]
-            grad = jnp.dot(cot_t[...], right, preferred_element_type=jnp.float32) * scale
-            if first == 0:
+            grad = jnp.dot(left, right, preferred_element_type=jnp.float32) * scale
+            if first == 0 and turns[0] == 0:
                 load_mem[h].wait()
                 if h == 0:
                     late.extend(later())
-            for j, c in enumerate(these):
-                view = pl.ds(c, all_rows, stride=tiles)
-                pend[h][view, :] = pend[h][view, :] + grad[:, j * LANES : (j + 1) * LANES]
+            for place, turn in enumerate(turns):
+                base = pl.multiple_of(owner_at(turn) * own, 8)
+                for j, c in enumerate(these):
+                    view = pl.ds(base + c, rows, stride=tiles)
+                    pend[h][view, :] = (
+                        pend[h][view, :]
+                        + grad[place * rows : (place + 1) * rows, j * LANES : (j + 1) * LANES]
+                    )
 
     def gather(owner, h):
         blocks = pend[h].at[pl.ds(pl.multiple_of(owner * own, 8), own)]
         for k in range(cap):
             slots[h, owner, pl.ds(k, 1), :] = blocks[pl.ds(kept_s[owner, k], 1), :]
 
-    pairs = shards // 2
     sends = []
     for h in range(halves):
-        multiply(h)
-        if h == 0:
-            load_kept_s.wait()
-        if h == 0:
-            pl.semaphore_wait(barrier, shards + 1)
         sends.append([])
-        for far, side in ((2, 1), (1, 0), (3, 0), (1, 1), (3, 1), (2, 0), (0, 1), (0, 0)):
-            owner = 2 * lax.rem(lax.div(shard, 2) + far, pairs) + lax.rem(shard + side, 2)
-            gather(owner, h)
-            step = 2 * far + side
-            if step:
-                copy = remote(
-                    slots.at[h, owner], arrived.at[h, shard], send_sem.at[h, step],
-                    recv_sem.at[h, step], (silo, owner),
-                )
-                copy.start()
-                sends[h].append(copy)
-            else:
-                arrived[h, shard] = slots[h, shard]
+        for turns in (range(pairs), range(pairs, shards)):
+            multiply(h, turns)
+            if h == 0 and turns[0] == 0:
+                load_kept_s.wait()
+                enter()
+            for turn in turns:
+                owner = owner_at(turn)
+                gather(owner, h)
+                if turn < shards - 1:
+                    copy = remote(
+                        slots.at[h, owner], arrived.at[h, shard], send_sem.at[h, turn],
+                        recv_sem.at[h, turn], (silo, owner),
+                    )
+                    copy.start()
+                    sends[h].append(copy)
+                else:
+                    arrived[h, shard] = slots[h, shard]
 
     for copy in late:
         copy.wait()
@@ -239,6 +282,7 @@
         return carry
 
     lax.fori_loop(0, shards, clear, 0)
+    await_near()
     for h in range(halves):
         settle(h)
         update(h)
@@ -321,10 +365,11 @@
             pltpu.SMEM((shards, shards), i32),
             pltpu.SMEM((1, silos), i32),
             pltpu.SemaphoreType.DMA((2 + halves * (tiles + 1) + 7,)),
-            pltpu.SemaphoreType.DMA((halves, shards)),
-            pltpu.SemaphoreType.DMA((halves, shards)),
+            pltpu.SemaphoreType.DMA((halves, shards - 1)),
+            pltpu.SemaphoreType.DMA((halves, shards - 1)),
             pltpu.SemaphoreType.DMA((halves, 2)),
             pltpu.SemaphoreType.DMA((halves, 2)),
+            pltpu.SemaphoreType.REGULAR,
         ],
         compiler_params=pltpu.CompilerParams(
             collective_id=0, has_side_effects=True, vmem_limit_bytes=24 << 20

time: 25.5 us -> 24.1 us (0.945)
  the two profiles are of different devices: /device:TPU:6 before, /device:TPU:16 now
where the time goes in v4:
time: 24.1 us; the launch traced here: 24 us
  Pallas kernels  23.4 us (97%)
  between operations  0.64 us (3%)
    pallas_call x1, Pallas kernels, body(): pl.pallas_call(functools.partial(kernel, dims), out_shape=(vmem((rows, wi...  21.2 us
    pallas_call x1, Pallas kernels, body(): pl.pallas_call(finish, out_shape=tuple((jax.ShapeDtypeStruct(x.shape, x.d...  2.15 us

profile of v4, /device:TPU:16, one launch (start us, length us, event | category | flops | bytes accessed | tf_op | source)
XLA Modules:
  0.0 24.0 jit_solution(14942200974554994816)
XLA Ops:
  0.6 21.2 %shard_map.129 = (f32[80,1280]{1,0:T(8,128)S(1)}, f32[80,1280]{1,0:T(8,128)S(1)}, f32[80,1280]{1,0:T(8,128)S(1)}, f32[3200,256]{1,0:T(8,128)S(1)}) custom-call(bf16[1024,1280]{1,0:T(8,128)(2,1)} %activ_h.1, bf16[1024,640]{1,0:T(8,128)(2,1)} %cot_h.1, f32[3200,256]{1,0:T(8,128)} %bitcast.11, f32[80,1280]{1,0:T(8,128)} %bitcast.12, f32[80,1280]{1,0:T(8,128)} %bitcast.13, ...), custom_call_target="tpu_custom_call" | custom-call | tf_op jit(solution)/shard_map/pallas_call | solution.py:329
  21.9 2.2 %shard_map.130 = (f32[80,1280]{1,0:T(8,128)}, f32[80,1280]{1,0:T(8,128)}, f32[80,1280]{1,0:T(8,128)}, f32[3200,256]{1,0:T(8,128)}) custom-call(f32[80,1280]{1,0:T(8,128)S(1)} %get-tuple-element.12.refs_0_, f32[80,1280]{1,0:T(8,128)S(1)} %get-tuple-element.13.refs_1_, f32[80,1280]{1,0:T(8,128)S(1)} %get-tuple-element.14.refs_2_, ...), custom_call_target="tpu_custom_call" | custom-call | tf_op jit(solution)/shard_map/pallas_call | solution.py:378

commit v5 on v4

--- a/solution.py
+++ b/solution.py
@@ -46,6 +46,13 @@
     upper = lax.rem(silo + 1, silos)
     lower = lax.rem(silo + silos - 1, silos)
     scale = float(activ_h.shape[1]) ** -0.5
+    pairs = shards // 2
+    here, side = lax.div(shard, 2), lax.rem(shard, 2)
+
+    def owner_at(turn):
+        far = (turn + 1) % pairs
+        return 2 * lax.rem(here + far, pairs) + (1 - side if turn < pairs else side)
+
     count = [0]
 
     def load(src, dst):
@@ -57,16 +64,36 @@
     def lanes_of(c, h):
         return pl.ds(c * block + h * LANES, LANES)
 
+    def load_all(copies, whole):
+        sem = load_sem.at[count[0]]
+        count[0] += 1
+        for src, dst in copies:
+            pltpu.make_async_copy(src, dst, sem).start()
+        return pltpu.make_async_copy(whole[0], whole[1], sem)
+
     def load_half(h):
-        return [
-            load(activ_h.at[:, lanes_of(c, h)], act_v[h].at[:, pl.ds(c * LANES, LANES)])
-            for c in range(tiles)
-        ]
-
+        return load_all(
+            [
+                (activ_h.at[:, lanes_of(c, h)], act_v[h].at[:, pl.ds(c * LANES, LANES)])
+                for c in range(tiles)
+            ],
+            (activ_h.at[:, pl.ds(0, tiles * LANES)], act_v[h]),
+        )
+
+    def load_pend(h, turns):
+        lanes = pl.ds(h * LANES, LANES)
+        views = [pl.ds(pl.multiple_of(owner_at(turn) * own, 8), own) for turn in turns]
+        whole = pl.ds(0, len(turns) * own)
+        return load_all(
+            [(mem_h.at[view, lanes], pend[h].at[view]) for view in views],
+            (mem_h.at[whole, lanes], pend[h].at[whole]),
+        )
+
+    parts = (range(pairs), range(pairs, shards))
     load_cot = load(cot_h, cot_v)
     load_act = [load_half(0)]
     load_kept_s = load(kept_h.at[shard], kept_s)
-    load_mem = [load(mem_h.at[:, pl.ds(0, LANES)], pend[0])]
+    load_mem = [[load_pend(0, turns) for turns in parts]]
 
     barrier = pltpu.get_barrier_semaphore()
     for step in range(1, shards):
@@ -101,13 +128,6 @@
             pl.semaphore_wait(near_sem, jnp.where(silo == 0, 2, 1))
 
     load_cot.wait()
-    pairs = shards // 2
-    here, side = lax.div(shard, 2), lax.rem(shard, 2)
-
-    def owner_at(turn):
-        far = (turn + 1) % pairs
-        return 2 * lax.rem(here + far, pairs) + (1 - side if turn < pairs else side)
-
     turned = cot_v[...].T
     for owner in range(shards):
         turn = lax.rem(owner // 2 - here + 2 * pairs - 1, pairs) + jnp.where(
@@ -122,7 +142,7 @@
     def later():
         for h in range(1, halves):
             load_act.append(load_half(h))
-            load_mem.append(load(mem_h.at[:, pl.ds(h * LANES, LANES)], pend[h]))
+            load_mem.append([load_pend(h, turns) for turns in parts])
         return [
             load(kept_h, kept_v),
             load(kcnt_h, kcnt_s),
@@ -135,15 +155,14 @@
 
     def multiply(h, turns):
         if turns[0] == 0:
-            for copy in load_act[h]:
-                copy.wait()
+            load_act[h].wait()
         left = cot_t[turns[0] * rows : (turns[-1] + 1) * rows, :]
         for first in range(0, tiles, 2):
             these = range(first, min(first + 2, tiles))
             right = act_v[h][:, pl.ds(first * LANES, len(these) * LANES)]
             grad = jnp.dot(left, right, preferred_element_type=jnp.float32) * scale
             if first == 0 and turns[0] == 0:
-                load_mem[h].wait()
+                load_mem[h][0].wait()
                 if h == 0:
                     late.extend(later())
             for place, turn in enumerate(turns):
@@ -163,8 +182,10 @@
     sends = []
     for h in range(halves):
         sends.append([])
-        for turns in (range(pairs), range(pairs, shards)):
+        for turns in parts:
             multiply(h, turns)
+            if turns[0] == 0:
+                load_mem[h][1].wait()
             if h == 0 and turns[0] == 0:
                 load_kept_s.wait()
                 enter()
@@ -286,9 +307,11 @@
     for h in range(halves):
         settle(h)
         update(h)
+    for copy in [copy for group in sends for copy in group]:
+        copy.wait_send()
     for h in range(halves):
         close(h)
-    for copy in [copy for group in sends for copy in group] + goes:
+    for copy in goes:
         copy.wait_send()
 
 
@@ -364,7 +387,7 @@
             pltpu.SMEM((shards, cap), i32),
             pltpu.SMEM((shards, shards), i32),
             pltpu.SMEM((1, silos), i32),
-            pltpu.SemaphoreType.DMA((2 + halves * (tiles + 1) + 7,)),
+            pltpu.SemaphoreType.DMA((2 + halves * 3 + 7,)),
             pltpu.SemaphoreType.DMA((halves, shards - 1)),
             pltpu.SemaphoreType.DMA((halves, shards - 1)),
             pltpu.SemaphoreType.DMA((halves, 2)),

time: 24.1 us -> 24 us (level)
  no operation moved by 1% of the time
where the time goes in v5:
time: 24 us; the launch traced here: 23.9 us
  Pallas kernels  23.2 us (97%)
  between operations  0.64 us (3%)
    pallas_call x1, Pallas kernels, body(): pl.pallas_call(functools.partial(kernel, dims), out_shape=(vmem((rows, wi...  21.1 us
    pallas_call x1, Pallas kernels, body(): pl.pallas_call(finish, out_shape=tuple((jax.ShapeDtypeStruct(x.shape, x.d...  2.15 us

profile of v5, /device:TPU:16, one launch (start us, length us, event | category | flops | bytes accessed | tf_op | source)
XLA Modules:
  0.0 23.9 jit_solution(5896791897725055732)
XLA Ops:
  0.6 21.1 %shard_map.129 = (f32[80,1280]{1,0:T(8,128)S(1)}, f32[80,1280]{1,0:T(8,128)S(1)}, f32[80,1280]{1,0:T(8,128)S(1)}, f32[3200,256]{1,0:T(8,128)S(1)}) custom-call(bf16[1024,1280]{1,0:T(8,128)(2,1)} %activ_h.1, bf16[1024,640]{1,0:T(8,128)(2,1)} %cot_h.1, f32[3200,256]{1,0:T(8,128)} %bitcast.11, f32[80,1280]{1,0:T(8,128)} %bitcast.12, f32[80,1280]{1,0:T(8,128)} %bitcast.13, ...), custom_call_target="tpu_custom_call" | custom-call | tf_op jit(solution)/shard_map/pallas_call | solution.py:352
  21.7 2.2 %shard_map.130 = (f32[80,1280]{1,0:T(8,128)}, f32[80,1280]{1,0:T(8,128)}, f32[80,1280]{1,0:T(8,128)}, f32[3200,256]{1,0:T(8,128)}) custom-call(f32[80,1280]{1,0:T(8,128)S(1)} %get-tuple-element.12.refs_0_, f32[80,1280]{1,0:T(8,128)S(1)} %get-tuple-element.13.refs_1_, f32[80,1280]{1,0:T(8,128)S(1)} %get-tuple-element.14.refs_2_, ...), custom_call_target="tpu_custom_call" | custom-call | tf_op jit(solution)/shard_map/pallas_call | solution.py:401

commit v6 on v5

--- a/solution.py
+++ b/solution.py
@@ -91,24 +91,25 @@
 
     parts = (range(pairs), range(pairs, shards))
     load_cot = load(cot_h, cot_v)
+
+    barrier = pltpu.get_barrier_semaphore()
+    for turn in (1, 0, 2, 5, 3, 4, 6):
+        pl.semaphore_signal(
+            barrier, inc=1, device_id=(silo, owner_at(turn)), device_id_type=MESH
+        )
+    last = silos - 1
+
+    @pl.when(silo != last)
+    def _():
+        pl.semaphore_signal(barrier, inc=1, device_id=(upper, shard), device_id_type=MESH)
+
+    @pl.when(silo == 0)
+    def _():
+        pl.semaphore_signal(barrier, inc=1, device_id=(lower, shard), device_id_type=MESH)
+
     load_act = [load_half(0)]
     load_kept_s = load(kept_h.at[shard], kept_s)
     load_mem = [[load_pend(0, turns) for turns in parts]]
-
-    barrier = pltpu.get_barrier_semaphore()
-    for step in range(1, shards):
-        pl.semaphore_signal(
-            barrier, inc=1, device_id=(silo, lax.rem(shard + step, shards)), device_id_type=MESH
-        )
-    last = silos - 1
-
-    @pl.when(silo != last)
-    def _():
-        pl.semaphore_signal(barrier, inc=1, device_id=(upper, shard), device_id_type=MESH)
-
-    @pl.when(silo == 0)
-    def _():
-        pl.semaphore_signal(barrier, inc=1, device_id=(lower, shard), device_id_type=MESH)
 
     def enter():
         greeted = jnp.where(silo == 0, 0, jnp.where(silo == last, 2, 1))
@@ -244,6 +245,8 @@
         gos_base[h] = taken[:, :LANES] + taken[:, LANES:]
 
     goes = []
+    quarter = lax.rem(silo, 4)
+    long_way = (quarter == 0) | (quarter == 3)
 
     def settle(h):
         for copy in sends[h]:
@@ -253,13 +256,19 @@
         pieces[h, :, pl.ds(LANES, LANES)] = low
         taken = jnp.dot(gos_mix[...], pieces[h], preferred_element_type=jnp.float32)
         gos_send[h] = gos_base[h] - LEARN_RATE * (taken[:, :LANES] + taken[:, LANES:])
-        for place, target in ((0, upper), (1, lower)):
-            copy = remote(
-                gos_send.at[h], gos_recv.at[h, place], gsend_sem.at[h, place],
-                grecv_sem.at[h, place], (target, shard),
+        odd = lax.rem(silo, 2)
+        for place, target in (
+            (1 - odd, jnp.where(odd == 1, upper, lower)),
+            (odd, jnp.where(odd == 1, lower, upper)),
+        ):
+            goes.append(
+                remote(
+                    gos_send.at[h], gos_recv.at[h, place], gsend_sem.at[h, place],
+                    grecv_sem.at[h, place], (target, shard),
+                )
             )
-            copy.start()
-            goes.append(copy)
+        pl.when(long_way)(goes[2 * h].start)
+        goes[2 * h + 1].start()
 
     def update(h):
         added = jnp.dot(onehot[...], pieces[h], preferred_element_type=jnp.float32)
@@ -307,6 +316,7 @@
     for h in range(halves):
         settle(h)
         update(h)
+        pl.when(jnp.logical_not(long_way))(goes[2 * h].start)
     for copy in [copy for group in sends for copy in group]:
         copy.wait_send()
     for h in range(halves):

time: 24 us -> 24.2 us (level)
  no operation moved by 1% of the time
where the time goes in v6:
time: 24.2 us; the launch traced here: 24 us
  Pallas kernels  23.4 us (97%)
  between operations  0.64 us (3%)
    pallas_call x1, Pallas kernels, body(): pl.pallas_call(functools.partial(kernel, dims), out_shape=(vmem((rows, wi...  21.2 us
    pallas_call x1, Pallas kernels, body(): pl.pallas_call(finish, out_shape=tuple((jax.ShapeDtypeStruct(x.shape, x.d...  2.15 us

profile of v6, /device:TPU:16, one launch (start us, length us, event | category | flops | bytes accessed | tf_op | source)
XLA Modules:
  0.0 24.0 jit_solution(1187985165345155658)
XLA Ops:
  0.6 21.2 %shard_map.129 = (f32[80,1280]{1,0:T(8,128)S(1)}, f32[80,1280]{1,0:T(8,128)S(1)}, f32[80,1280]{1,0:T(8,128)S(1)}, f32[3200,256]{1,0:T(8,128)S(1)}) custom-call(bf16[1024,1280]{1,0:T(8,128)(2,1)} %activ_h.1, bf16[1024,640]{1,0:T(8,128)(2,1)} %cot_h.1, f32[3200,256]{1,0:T(8,128)} %bitcast.11, f32[80,1280]{1,0:T(8,128)} %bitcast.12, f32[80,1280]{1,0:T(8,128)} %bitcast.13, ...), custom_call_target="tpu_custom_call" | custom-call | tf_op jit(solution)/shard_map/pallas_call | solution.py:362
  21.9 2.2 %shard_map.130 = (f32[80,1280]{1,0:T(8,128)}, f32[80,1280]{1,0:T(8,128)}, f32[80,1280]{1,0:T(8,128)}, f32[3200,256]{1,0:T(8,128)}) custom-call(f32[80,1280]{1,0:T(8,128)S(1)} %get-tuple-element.12.refs_0_, f32[80,1280]{1,0:T(8,128)S(1)} %get-tuple-element.13.refs_1_, f32[80,1280]{1,0:T(8,128)S(1)} %get-tuple-element.14.refs_2_, ...), custom_call_target="tpu_custom_call" | custom-call | tf_op jit(solution)/shard_map/pallas_call | solution.py:411
